TPU v7x, 1024 devices: a whole 8x8x8 slice. The times are simulated.
1024 devices in a mesh: pipe: 8 (over y), dp: 8 (over z), expert: 16 (over x, core).
Axes of the slice: x: 8, y: 8, z: 8, core: 2. Of those that a mesh axis runs over, the one named last changes fastest.
Arguments:
- input_grad: bfloat16 [8, 16384, 2048], P('pipe', ('dp', 'expert')), may hold values from -0.75 to 0.75
- gate_prob: float32 [8, 16384], P('pipe', ('dp', 'expert')), may hold values from 0.2 to 1
- expert_route: int32 [8, 16384, 1], P('pipe', ('dp', 'expert')), may hold values from 0 to 7; in each aligned block of 128 rows (0 to 127, 128 to 255, ..., all dimensions but the last counted through in order) at most 32 rows name the same one
- saved_hidden: bfloat16 [8, 8, 16, 32, 22528], P('pipe', 'dp', None, None, 'expert'), may hold values from -6 to 6
Outputs:
- down_grad: bfloat16 [8, 2048, 22528], P('pipe', 'dp', 'expert')
Inputs may be any that keep to these rules, and one draw needn't show every extreme that they name: `expert_route`: among the 128 tokens of one index of dp and expert no expert is named more than 32 times, and in every draw some expert is named exactly 32 times by some device's tokens.
All inputs are finite; a program needn't handle non-finite values.
Results may differ from a plain program's by a relative error of at most 0.014.
Values may be sent and summed in bfloat16 or wider, within the bound.
A program may use at most 32 MiB of HBM per device.

v0:
```python
import jax
import jax.numpy as jnp
from jax import lax
from jax.sharding import PartitionSpec as P


def shifted(value, axis, steps):
    count = lax.axis_size(axis)
    pairs = [(source, (source + steps) % count) for source in range(count)]
    return lax.ppermute(value, axis, pairs)


def body(input_grad, gate_prob, expert_route, saved_hidden):
    grad_rows = shifted(input_grad, "pipe", -1)[0]
    flight_count = lax.axis_size("expert") // 2
    capacity = saved_hidden.shape[3]
    token_count = grad_rows.shape[0]
    model_width = grad_rows.shape[1]
    routes = expert_route[0, :, 0]
    one_hot = (routes[:, None] == jnp.arange(flight_count, dtype=jnp.int32)[None, :]).astype(
        jnp.float32
    )
    row_ids = lax.broadcasted_iota(jnp.int32, (token_count, token_count), 0)
    column_ids = lax.broadcasted_iota(jnp.int32, (token_count, token_count), 1)
    earlier_mask = (column_ids < row_ids).astype(jnp.float32)
    before = jnp.dot(earlier_mask, one_hot, precision=lax.Precision.HIGHEST)
    position = jnp.sum(before * one_hot, axis=1)
    slot_values = jnp.arange(capacity, dtype=jnp.float32)
    slot_hit = one_hot[:, :, None] * (position[:, None, None] == slot_values[None, None, :]).astype(
        jnp.float32
    )
    scaled = (gate_prob[0][:, None] * grad_rows.astype(jnp.float32)).astype(jnp.bfloat16)
    outgoing = jnp.einsum(
        "tec,td->ecd", slot_hit.astype(jnp.bfloat16), scaled, preferred_element_type=jnp.float32
    ).astype(jnp.bfloat16)
    copies = jnp.broadcast_to(outgoing[:, None], (flight_count, 2, capacity, model_width))
    copies = copies.reshape(2 * flight_count, capacity, model_width)
    received = lax.all_to_all(copies, "expert", split_axis=0, concat_axis=0, tiled=True)
    source_count = received.shape[0]
    flat_rows = received.reshape(source_count * capacity, model_width)
    hidden = saved_hidden.reshape(source_count * capacity, saved_hidden.shape[4])
    summed = lax.psum_scatter(
        lax.dot_general(
            flat_rows, hidden, (((0,), (0,)), ((), ())), preferred_element_type=jnp.float32
        ).astype(jnp.bfloat16),
        "dp",
        scatter_dimension=0,
        tiled=True,
    )
    return summed[None]


def solution(mesh):
    in_specs = (
        P("pipe", ("dp", "expert"), None),
        P("pipe", ("dp", "expert")),
        P("pipe", ("dp", "expert"), None),
        P("pipe", "dp", None, None, "expert"),
    )
    out_specs = P("pipe", "dp", "expert")
    return jax.shard_map(body, mesh=mesh, in_specs=in_specs, out_specs=out_specs, check_vma=False)
```

profile of v0, /device:TPU:1, one launch (start us, length us, event | category | flops | bytes accessed | tf_op | source)
XLA Modules:
  0.0 179.5 jit_solution(9241984524504672420)
XLA Ops:
  6.5 0.0 copy-start
  6.5 0.0 reduce-scatter.2.cloned.1.call-start
  6.5 6.8 %collective-permute-start = (bf16[1,128,2048]{2,1,0:T(8,128)(2,1)}, bf16[1,128,2048]{2,1,0:T(8,128)(2,1)S(1)}, u32[]{:S(2)}, u32[]{:S(2)}) collective-permute-start(bf16[1,128,2048]{2,1,0:T(8,128)(2,1)} %param.4), channel_id=1, source_target_pairs={{0,896},{128,0},{256,128},{384,256},{512,384},{640,512},{768,640},... | collective-permute-start | bytes 1572872 | tf_op jit(solution)/shard_map/ppermute | solution.py:10
  13.4 0.9 fusion
  14.3 0.7 fusion.9
  14.9 4.8 %collective-permute-done = bf16[1,128,2048]{2,1,0:T(8,128)(2,1)S(1)} collective-permute-done((bf16[1,128,2048]{2,1,0:T(8,128)(2,1)}, bf16[1,128,2048]{2,1,0:T(8,128)(2,1)S(1)}, u32[]{:S(2)}, u32[]{:S(2)}) %collective-permute-start) | collective-permute-done | bytes 524320 | tf_op jit(solution)/shard_map/ppermute | solution.py:10
  19.8 1.1 convolution_convert_fusion.1
  20.9 0.3 broadcast_in_dim.4
  21.2 65.7 %all_to_all.5 = bf16[16,32,2048]{2,1,0:T(8,128)(2,1)S(1)} all-to-all(bf16[16,32,2048]{2,1,0:T(8,128)(2,1)S(1)} %bitcast.18), channel_id=1, replica_groups=mesh['pipe'=8,'dp'=8,'expert'=16] {'expert'}, dimensions={0} | all-to-all | bytes 4194304 | tf_op jit(solution)/shard_map/all_to_all | solution.py:38
  86.9 0.0 copy-done
  86.9 5.3 %convolution_convert_fusion = bf16[2048,1408]{1,0:T(8,128)(2,1)} fusion(bf16[512,2048]{1,0:T(8,128)(2,1)S(1)} %bitcast.19, bf16[512,1408]{1,0:T(8,128)(2,1)S(1)} %bitcast.17), kind=kOutput, calls=%fused_computation | convolution fusion | flops 2955673600 | bytes 9306112 | tf_op jit(solution)/shard_map/dot_general | solution.py:43
  92.3 0.0 reduce-scatter.2.cloned.1.call-update
  92.3 80.3 %reduce-scatter.2.cloned.1.call-done = bf16[256,1408]{1,0:T(8,128)(2,1)} async-done(((bf16[2048,1408]{1,0:T(8,128)(2,1)}), bf16[256,1408]{1,0:T(8,128)(2,1)}) %reduce-scatter.2.cloned.1.call-update) | async-done | bytes 720912 | tf_op jit(solution)/shard_map/reduce_scatter | solution.py:42
  (1 shorter events, 0.0 us)
Async XLA Ops:
  6.5 80.4 %copy-start = (bf16[1,1,16,32,1408]{4,3,2,1,0:T(8,128)(2,1)S(1)}, bf16[1,1,16,32,1408]{4,3,2,1,0:T(8,128)(2,1)}, u32[]{:S(2)}) copy-start(bf16[1,1,16,32,1408]{4,3,2,1,0:T(8,128)(2,1)} %param.7) | copy-start | bytes 4325380
  6.5 166.1 %reduce-scatter.2.cloned.1.call-start = ((), (), s32[]{:S(2)}) async-start(), calls=%async_computation.2 | async-start | bytes 6488064 | tf_op jit(solution)/shard_map/reduce_scatter | solution.py:42
  6.5 13.3 %collective-permute-start = (bf16[1,128,2048]{2,1,0:T(8,128)(2,1)}, bf16[1,128,2048]{2,1,0:T(8,128)(2,1)S(1)}, u32[]{:S(2)}, u32[]{:S(2)}) collective-permute-start(bf16[1,128,2048]{2,1,0:T(8,128)(2,1)} %param.4), channel_id=1, source_target_pairs={{0,896},{128,0},{256,128},{384,256},{512,384},{640,512},{768,640},... | collective-permute-start | bytes 1572872 | tf_op jit(solution)/shard_map/ppermute | solution.py:10
Sparse Core Ops, SparseCore 0:
  92.4 80.1 reduce-scatter.1
where the time goes:
time: 180 us; the launch traced here: 179 us
  waiting for transfers between devices  85.2 us (47%)
  blocking collectives  65.7 us (36%)
  between operations  13.4 us (7%)
  matrix products  7.37 us (4%)
  starting transfers between devices  6.83 us (4%)
    reduce_scatter x1, waiting for transfers between devices, body(): lax.psum_scatter(lax.dot_general(flat_rows, hidden, (((0,), (0,)), ((), (...  80.3 us
    all_to_all x1, blocking collectives, body(): lax.all_to_all(copies, 'expert', split_axis=0, concat_axis=0, tiled=True)  65.7 us
    ppermute x1, starting transfers between devices, shifted(): return lax.ppermute(value, axis, pairs)  6.83 us
    dot_general x1, matrix products, body(): lax.dot_general(flat_rows, hidden, (((0,), (0,)), ((), ())), preferred_el...  5.34 us
    ppermute x1, waiting for transfers between devices, shifted(): return lax.ppermute(value, axis, pairs)  4.85 us
  transfers between devices with their start and end apart: 2, of which 2 were waited for; matrix products, arithmetic and copies ran while one was open for 1% of the time, Pallas kernels for 0%

commit v1 on v0

v1 whole, which is shorter than its diff:
```python
import functools

import jax
import jax.numpy as jnp
from jax import lax
from jax.experimental import pallas as pl
from jax.experimental.pallas import tpu as pltpu
from jax.sharding import PartitionSpec as P

MESH = pl.DeviceIdType.MESH


def kernel(
    sizes,
    grad_ref,
    prob_ref,
    route_ref,
    hidden_ref,
    out_ref,
    grad_in,
    outgoing,
    received,
    part,
    from_left,
    from_right,
    hidden,
    prob,
    route,
    select,
    prob_column,
    local_sems,
    grad_send,
    grad_recv,
    rows_send,
    rows_recv,
    own_sems,
    share_send,
    share_recv,
    right_send,
    right_recv,
    left_send,
    left_recv,
):
    n_pipe, n_dp, n_chip = sizes
    tokens, width = grad_ref.shape[1:]
    flights, capacity = outgoing.shape[1:3]
    blocks = n_dp
    columns = width // blocks
    half = columns // 2
    far = n_dp // 2

    section = lax.axis_index("pipe")
    replica = lax.axis_index("dp")
    index = lax.axis_index("expert")
    chip, core = index // 2, index % 2

    def along_dp(offset):
        return lax.rem(replica + offset + n_dp, n_dp)

    before = {"pipe": lax.rem(section + n_pipe - 1, n_pipe)}
    after = {"pipe": lax.rem(section + 1, n_pipe)}
    right = {"dp": along_dp(1)}
    left = {"dp": along_dp(-1)}
    sibling = {"expert": chip * 2 + 1 - core}

    def on_chip(distance):
        return lax.rem(chip + distance, n_chip)

    def peer(distance):
        return {"expert": on_chip(distance) * 2 + core}

    offsets = [far]
    for distance in range(far - 1, 0, -1):
        offsets += [distance, -distance]
    offsets.append(0)

    hidden_copy = pltpu.make_async_copy(hidden_ref.at[0, 0], hidden, local_sems.at[0])
    prob_copy = pltpu.make_async_copy(prob_ref, prob, local_sems.at[1])
    route_copy = pltpu.make_async_copy(route_ref, route, local_sems.at[2])
    hidden_copy.start()
    prob_copy.start()
    route_copy.start()

    barrier = pltpu.get_barrier_semaphore()
    partners = [before, after, right, left, sibling] + [peer(d) for d in range(1, n_chip)]
    for partner in partners:
        pl.semaphore_signal(barrier, inc=1, device_id=partner, device_id_type=MESH)
    pl.semaphore_wait(barrier, len(partners))

    def grad_copy(j):
        start = pl.multiple_of(along_dp(offsets[j]) * columns, columns)
        return pltpu.make_async_remote_copy(
            src_ref=grad_ref.at[0, :, pl.ds(start, columns)],
            dst_ref=grad_in.at[j],
            send_sem=grad_send.at[j],
            recv_sem=grad_recv.at[j],
            device_id=before,
            device_id_type=MESH,
        )

    grad_copies = [grad_copy(j) for j in range(blocks)]
    for copy in grad_copies:
        copy.start()

    prob_copy.wait()
    route_copy.wait()
    routes = route[...]
    flight_ids = lax.broadcasted_iota(jnp.int32, (flights, tokens), 0)
    one_hot = (flight_ids == routes).astype(jnp.float32)
    rows_of = lax.broadcasted_iota(jnp.int32, (tokens, tokens), 0)
    columns_of = lax.broadcasted_iota(jnp.int32, (tokens, tokens), 1)
    earlier = jnp.dot(
        one_hot.astype(jnp.bfloat16),
        (rows_of < columns_of).astype(jnp.bfloat16),
        preferred_element_type=jnp.float32,
    )
    position = jnp.sum(earlier * one_hot, axis=0, keepdims=True)
    place = routes * capacity + position.astype(jnp.int32)
    slot_ids = lax.broadcasted_iota(jnp.int32, (flights * capacity, tokens), 0)
    select[...] = (slot_ids == place).astype(jnp.float32).astype(jnp.bfloat16)
    diagonal = jnp.where(rows_of == columns_of, jnp.broadcast_to(prob[...], (tokens, tokens)), 0.0)
    prob_column[...] = jnp.broadcast_to(
        jnp.sum(diagonal, axis=1, keepdims=True), prob_column.shape
    )

    def rows_copy(j, distance):
        return pltpu.make_async_remote_copy(
            src_ref=outgoing.at[j, on_chip(distance)],
            dst_ref=received.at[j, chip, core],
            send_sem=rows_send.at[j],
            recv_sem=rows_recv.at[j],
            device_id=peer(distance),
            device_id_type=MESH,
        )

    def own_copy(j):
        return pltpu.make_async_copy(
            outgoing.at[j, chip], received.at[j, chip, core], own_sems.at[j]
        )

    def share_copy(j):
        return pltpu.make_async_remote_copy(
            src_ref=received.at[j, :, core],
            dst_ref=received.at[j, :, core],
            send_sem=share_send.at[j],
            recv_sem=share_recv.at[j],
            device_id=sibling,
            device_id_type=MESH,
        )

    def dispatch(j):
        grad_copies[j].wait_recv()
        scale = prob_column[...]
        for at in range(0, columns, scale.shape[1]):
            span = slice(at, at + scale.shape[1])
            scaled = (grad_in[j, :, span].astype(jnp.float32) * scale).astype(jnp.bfloat16)
            rows = jnp.dot(select[...], scaled, preferred_element_type=jnp.float32)
            outgoing[j, :, :, span] = rows.astype(jnp.bfloat16).reshape(
                flights, capacity, scale.shape[1]
            )
        for distance in (4, 3, 5, 2, 6, 1, 7):
            rows_copy(j, distance).start()
        own_copy(j).start()

    def share(j):
        own_copy(j).wait()
        taken = received.at[j, pl.ds(0, n_chip - 1), core]
        pltpu.make_async_copy(taken, taken, rows_recv.at[j]).wait()
        share_copy(j).start()

    def multiply(j):
        share_copy(j).wait_recv()
        rows = received[j].reshape(n_chip * 2 * capacity, columns)
        part[j] = lax.dot_general(
            rows, hidden[...], (((0,), (0,)), ((), ())), preferred_element_type=jnp.float32
        ).astype(jnp.bfloat16)

    steps = [(far, 0)]
    for distance in range(far - 1, 0, -1):
        steps += [(distance, 1), (distance, 0)]

    def chain(direction):
        to_right = direction > 0
        send, recv = (right_send, right_recv) if to_right else (left_send, left_recv)
        landing = from_left if to_right else from_right
        target = right if to_right else left
        places = []
        for distance, piece in steps:
            block = offsets.index(far if distance == far else direction * distance)
            places.append((block, piece if to_right else 1 - piece))

        def copy(n):
            block, piece = places[n]
            return pltpu.make_async_remote_copy(
                src_ref=part.at[block, pl.ds(piece * half, half)],
                dst_ref=landing.at[n],
                send_sem=send.at[n],
                recv_sem=recv.at[n],
                device_id=target,
                device_id_type=MESH,
            )

        def add(n):
            block, piece = places[n]
            span = pl.ds(piece * half, half)
            copy(n - 2).wait_recv()
            part[block, span] = (
                part[block, span].astype(jnp.float32) + landing[n - 2].astype(jnp.float32)
            ).astype(jnp.bfloat16)

        return copy, add

    right_copy, right_add = chain(1)
    left_copy, left_add = chain(-1)
    last = len(steps)

    def reduce_step(n):
        if n >= 2:
            right_add(n)
            right_copy(n).start()
            left_add(n)
            left_copy(n).start()
        else:
            right_copy(n).start()
            left_copy(n).start()

    dispatch(0)
    hidden_copy.wait()
    dispatch(1)
    dispatch(2)
    dispatch(3)
    share(0)
    dispatch(4)
    multiply(0)
    reduce_step(0)
    for j in range(5, blocks):
        dispatch(j)
    share(1)
    share(2)
    multiply(1)
    multiply(2)
    reduce_step(1)
    reduce_step(2)
    for j in range(3, blocks - 1, 2):
        share(j)
        share(j + 1)
        multiply(j)
        multiply(j + 1)
        reduce_step(j)
        reduce_step(j + 1)
    share(blocks - 1)
    multiply(blocks - 1)

    own = part.at[blocks - 1]
    pieces = [pl.ds(0, half), pl.ds(half, half)]
    right_copy(last - 2).wait_recv()
    left_copy(last - 2).wait_recv()
    for span, landing in ((pieces[1], from_left), (pieces[0], from_right)):
        own[span] = (
            own[span].astype(jnp.float32) + landing[last - 2].astype(jnp.float32)
        ).astype(jnp.bfloat16)
    right_copy(last - 1).wait_recv()
    left_copy(last - 1).wait_recv()
    for span, landing in ((pieces[0], from_left), (pieces[1], from_right)):
        out_ref[0, span] = (
            own[span].astype(jnp.float32) + landing[last - 1].astype(jnp.float32)
        ).astype(jnp.bfloat16)

    for j in range(blocks):
        grad_copies[j].wait_send()
        sent = outgoing.at[j, pl.ds(0, n_chip - 1)]
        pltpu.make_async_copy(sent, sent, rows_send.at[j]).wait()
        share_copy(j).wait_send()
    for n in range(last):
        right_copy(n).wait_send()
        left_copy(n).wait_send()


def solution(mesh):
    sizes = (mesh.shape["pipe"], mesh.shape["dp"], mesh.shape["expert"] // 2)
    n_dp, n_chip = sizes[1:]

    def body(input_grad, gate_prob, expert_route, saved_hidden):
        tokens, width = input_grad.shape[1:]
        capacity, hidden_width = saved_hidden.shape[3:]
        rows = saved_hidden.shape[2] * capacity
        columns = width // n_dp
        half = columns // 2
        chain_steps = n_dp - 1
        dma = pltpu.SemaphoreType.DMA
        anywhere = pl.BlockSpec(memory_space=pl.ANY)
        result = pl.pallas_call(
            functools.partial(kernel, sizes),
            out_shape=jax.ShapeDtypeStruct((1, columns, hidden_width), jnp.bfloat16),
            in_specs=[anywhere] * 4,
            out_specs=pl.BlockSpec(memory_space=pltpu.VMEM),
            scratch_shapes=[
                pltpu.VMEM((n_dp, tokens, columns), jnp.bfloat16),
                pltpu.VMEM((n_dp, n_chip, capacity, columns), jnp.bfloat16),
                pltpu.VMEM((n_dp, n_chip, 2, capacity, columns), jnp.bfloat16),
                pltpu.VMEM((n_dp, columns, hidden_width), jnp.bfloat16),
                pltpu.VMEM((chain_steps, half, hidden_width), jnp.bfloat16),
                pltpu.VMEM((chain_steps, half, hidden_width), jnp.bfloat16),
                pltpu.VMEM((rows, hidden_width), jnp.bfloat16),
                pltpu.VMEM((1, tokens), jnp.float32),
                pltpu.VMEM((1, tokens), jnp.int32),
                pltpu.VMEM((n_chip * capacity, tokens), jnp.bfloat16),
                pltpu.VMEM((tokens, 128), jnp.float32),
                dma((3,)),
                dma((n_dp,)),
                dma((n_dp,)),
                dma((n_dp,)),
                dma((n_dp,)),
                dma((n_dp,)),
                dma((n_dp,)),
                dma((n_dp,)),
                dma((chain_steps,)),
                dma((chain_steps,)),
                dma((chain_steps,)),
                dma((chain_steps,)),
            ],
            compiler_params=pltpu.CompilerParams(
                collective_id=0, has_side_effects=True, vmem_limit_bytes=60 * 1024 * 1024
            ),
        )(
            input_grad,
            gate_prob,
            expert_route.reshape(1, tokens),
            saved_hidden.reshape(1, 1, rows, hidden_width),
        )
        return result

    in_specs = (
        P("pipe", ("dp", "expert"), None),
        P("pipe", ("dp", "expert")),
        P("pipe", ("dp", "expert"), None),
        P("pipe", "dp", None, None, "expert"),
    )
    out_specs = P("pipe", "dp", "expert")
    return jax.shard_map(body, mesh=mesh, in_specs=in_specs, out_specs=out_specs, check_vma=False)
```

time: 180 us -> 94 us (0.52)
  Pallas kernels: 0 us -> 91.4 us
  waiting for transfers between devices: 85.2 us -> 0 us
  blocking collectives: 65.7 us -> 0 us
  between operations: 13.4 us -> 0.01 us
  matrix products: 7.37 us -> 0 us
  starting transfers between devices: 6.83 us -> 0 us
    pallas_call x0 -> x1, Pallas kernels: none -> 91.4 us  [body(): pl.pallas_call(functools.partial(kernel, sizes), out_shape=jax.ShapeDtype...]
    reduce_scatter x1 -> x0, waiting for transfers between devices: 80.3 us -> none  [body(): lax.psum_scatter(lax.dot_general(flat_rows, hidden, (((0,), (0,)), ((), (...]
    all_to_all x1 -> x0, blocking collectives: 65.7 us -> none  [body(): lax.all_to_all(copies, 'expert', split_axis=0, concat_axis=0, tiled=True)]
    dot_general x3 -> x0, matrix products: 7.37 us -> none  [the longest x1 5.34 us: body(): lax.dot_general(flat_rows, hidden, (((0,), (0,)), ((), ())), preferred_el...]
    ppermute x1 -> x0, starting transfers between devices: 6.83 us -> none  [shifted(): return lax.ppermute(value, axis, pairs)]
    ppermute x1 -> x0, waiting for transfers between devices: 4.85 us -> none  [shifted(): return lax.ppermute(value, axis, pairs)]
    unnamed x2 -> x1, local copies, waits for them, and re-layouts: 0.01 us -> 2.02 us
  transfers between devices with their start and end apart: 2 -> 0, of which waited for: 2 -> 0; matrix products, arithmetic and copies ran while one was open for 1% -> 0% of each run, Pallas kernels for 0% -> 0%
where the time goes in v1:
time: 94 us; the launch traced here: 93.4 us
  Pallas kernels  91.4 us (97%)
  local copies, waits for them, and re-layouts  2.02 us (2%)
    pallas_call x1, Pallas kernels, body(): pl.pallas_call(functools.partial(kernel, sizes), out_shape=jax.ShapeDtype...  91.4 us
    unnamed x1, local copies, waits for them, and re-layouts  2.02 us

profile of v1, /device:TPU:1, one launch (start us, length us, event | category | flops | bytes accessed | tf_op | source)
XLA Modules:
  0.0 93.4 jit_solution(4720881035640300386)
XLA Ops:
  0.0 91.4 %shard_map.46 = bf16[1,256,1408]{2,1,0:T(8,128)(2,1)} custom-call(bf16[1,128,2048]{2,1,0:T(8,128)(2,1)} %grad_ref.1, f32[1,128]{1,0:T(1,128)} %prob_ref.1, s32[1,128]{1,0:T(1,128)} %bitcast.3, bf16[1,1,512,1408]{3,2,1,0:T(8,128)(2,1)} %bitcast.2), custom_call_target="tpu_custom_call" | custom-call | tf_op jit(solution)/shard_map/pallas_call | solution.py:292
  91.4 2.0 %copy.6 = bf16[1,256,1408]{2,1,0:T(8,128)(2,1)} copy(bf16[1,256,1408]{2,1,0:T(8,128)(2,1)} %shard_map.46) | data formatting | bytes 1441792

commit v2 on v1

v2 whole, which is shorter than its diff:
```python
import functools

import jax
import jax.numpy as jnp
from jax import lax
from jax.experimental import pallas as pl
from jax.experimental.pallas import tpu as pltpu
from jax.sharding import PartitionSpec as P

MESH = pl.DeviceIdType.MESH


def kernel(
    sizes,
    grad_ref,
    prob_ref,
    route_ref,
    hidden_ref,
    out_ref,
    grad_in,
    outgoing,
    received,
    part,
    from_left,
    from_right,
    hidden,
    prob,
    route,
    select,
    prob_column,
    local_sems,
    grad_send,
    grad_recv,
    rows_send,
    rows_recv,
    own_sems,
    share_send,
    share_recv,
    right_send,
    right_recv,
    left_send,
    left_recv,
):
    n_pipe, n_dp, n_chip = sizes
    units, tokens, columns = grad_in.shape
    flights, capacity = outgoing.shape[1:3]
    cuts = units // n_dp
    half = columns // 2
    far = n_dp // 2

    section = lax.axis_index("pipe")
    replica = lax.axis_index("dp")
    index = lax.axis_index("expert")
    chip, core = index // 2, index % 2

    def along_dp(offset):
        return lax.rem(replica + offset + n_dp, n_dp)

    before = {"pipe": lax.rem(section + n_pipe - 1, n_pipe)}
    after = {"pipe": lax.rem(section + 1, n_pipe)}
    right = {"dp": along_dp(1)}
    left = {"dp": along_dp(-1)}
    sibling = {"expert": chip * 2 + 1 - core}

    def on_chip(distance):
        return lax.rem(chip + distance, n_chip)

    def peer(distance):
        return {"expert": on_chip(distance) * 2 + core}

    order = [(far, cut) for cut in range(cuts)]
    for distance in range(far - 1, 0, -1):
        order += [(side * distance, cut) for cut in range(cuts) for side in (1, -1)]
    order += [(0, cut) for cut in range(cuts)]

    hidden_copy = pltpu.make_async_copy(hidden_ref.at[0, 0], hidden, local_sems.at[0])
    prob_copy = pltpu.make_async_copy(prob_ref, prob, local_sems.at[1])
    route_copy = pltpu.make_async_copy(route_ref, route, local_sems.at[2])
    hidden_copy.start()
    prob_copy.start()
    route_copy.start()

    barrier = pltpu.get_barrier_semaphore()
    partners = [right, left, sibling] + [peer(d) for d in range(1, n_chip)]

    for partner in partners + [after]:
        pl.semaphore_signal(barrier, inc=1, device_id=partner, device_id_type=MESH)
    pl.semaphore_wait(barrier, len(partners) + 1)

    def grad_copy(u):
        distance, cut = order[u]
        start = pl.multiple_of((along_dp(distance) * cuts + cut) * columns, columns)
        return pltpu.make_async_remote_copy(
            src_ref=grad_ref.at[0, :, pl.ds(start, columns)],
            dst_ref=grad_in.at[u],
            send_sem=grad_send.at[u],
            recv_sem=grad_recv.at[u],
            device_id=before,
            device_id_type=MESH,
        )

    for u in range(units):
        grad_copy(u).start()

    prob_copy.wait()
    route_copy.wait()
    routes = route[...]
    flight_ids = lax.broadcasted_iota(jnp.int32, (flights, tokens), 0)
    one_hot = (flight_ids == routes).astype(jnp.float32)
    rows_of = lax.broadcasted_iota(jnp.int32, (tokens, tokens), 0)
    columns_of = lax.broadcasted_iota(jnp.int32, (tokens, tokens), 1)
    earlier = jnp.dot(
        one_hot.astype(jnp.bfloat16),
        (rows_of < columns_of).astype(jnp.bfloat16),
        preferred_element_type=jnp.float32,
    )
    position = jnp.sum(earlier * one_hot, axis=0, keepdims=True)
    place = routes * capacity + position.astype(jnp.int32)
    slot_ids = lax.broadcasted_iota(jnp.int32, (flights * capacity, tokens), 0)
    select[...] = (slot_ids == place).astype(jnp.float32).astype(jnp.bfloat16)
    diagonal = jnp.where(rows_of == columns_of, jnp.broadcast_to(prob[...], (tokens, tokens)), 0.0)
    prob_column[...] = jnp.broadcast_to(
        jnp.sum(diagonal, axis=1, keepdims=True), prob_column.shape
    )

    def rows_copy(u, distance):
        return pltpu.make_async_remote_copy(
            src_ref=outgoing.at[u, on_chip(distance)],
            dst_ref=received.at[u, chip, core],
            send_sem=rows_send.at[u],
            recv_sem=rows_recv.at[u],
            device_id=peer(distance),
            device_id_type=MESH,
        )

    def own_copy(u):
        return pltpu.make_async_copy(
            outgoing.at[u, chip], received.at[u, chip, core], own_sems.at[u]
        )

    def share_copy(u):
        return pltpu.make_async_remote_copy(
            src_ref=received.at[u, :, core],
            dst_ref=received.at[u, :, core],
            send_sem=share_send.at[u],
            recv_sem=share_recv.at[u],
            device_id=sibling,
            device_id_type=MESH,
        )

    far_first = sorted(range(1, n_chip), key=lambda d: -min(d, n_chip - d))

    def dispatch(u):
        grad_copy(u).wait_recv()
        scaled = (grad_in[u].astype(jnp.float32) * prob_column[...]).astype(jnp.bfloat16)
        rows = jnp.dot(select[...], scaled, preferred_element_type=jnp.float32)
        outgoing[u] = rows.astype(jnp.bfloat16).reshape(flights, capacity, columns)
        for distance in far_first:
            rows_copy(u, distance).start()
        own_copy(u).start()

    def share(u):
        own_copy(u).wait()
        taken = received.at[u, pl.ds(0, n_chip - 1), core]
        pltpu.make_async_copy(taken, taken, rows_recv.at[u]).wait()
        share_copy(u).start()

    def multiply(u):
        share_copy(u).wait_recv()
        rows = received[u].reshape(n_chip * 2 * capacity, columns)
        part[u] = lax.dot_general(
            rows, hidden[...], (((0,), (0,)), ((), ())), preferred_element_type=jnp.float32
        ).astype(jnp.bfloat16)

    steps = [(far, cut, 0, None) for cut in range(cuts)]
    for distance in range(far - 1, 0, -1):
        for cut in range(cuts):
            for piece in (1, 0):
                source = (distance + 1, cut, piece)
                known = [step[:3] for step in steps]
                steps.append(
                    (distance, cut, piece, known.index(source) if source in known else None)
                )
    last = len(steps)

    def chain(side):
        to_right = side > 0
        send, recv = (right_send, right_recv) if to_right else (left_send, left_recv)
        landing = from_left if to_right else from_right
        target = right if to_right else left

        def place_of(n, closer=0):
            distance, cut, piece, source = steps[n]
            distance -= closer
            unit = order.index((distance if distance == far else side * distance, cut))
            row = (piece if to_right else 1 - piece) * half
            return unit, row, source

        def copy(n):
            unit, row, _ = place_of(n)
            return pltpu.make_async_remote_copy(
                src_ref=part.at[unit, pl.ds(row, half)],
                dst_ref=landing.at[n],
                send_sem=send.at[n],
                recv_sem=recv.at[n],
                device_id=target,
                device_id_type=MESH,
            )

        def advance(n):
            unit, row, source = place_of(n)
            if source is not None:
                copy(source).wait_recv()
                part[unit, pl.ds(row, half)] = (
                    part[unit, pl.ds(row, half)].astype(jnp.float32)
                    + landing[source].astype(jnp.float32)
                ).astype(jnp.bfloat16)
            copy(n).start()

        def finish(n, to_out):
            unit, row, _ = place_of(n, closer=1)
            copy(n).wait_recv()
            total = (
                part[unit, pl.ds(row, half)].astype(jnp.float32) + landing[n].astype(jnp.float32)
            ).astype(jnp.bfloat16)
            if to_out:
                out_ref[0, pl.ds(steps[n][1] * columns + row, half)] = total
            else:
                part[unit, pl.ds(row, half)] = total

        return copy, advance, finish

    right_copy, right_advance, right_finish = chain(1)
    left_copy, left_advance, left_finish = chain(-1)

    def reduce_step(n):
        right_advance(n)
        left_advance(n)

    for u in range(units // 2):
        dispatch(u)
        if u == 0:
            hidden_copy.wait()
    waiting = list(range(units // 2, units))
    done = 0
    for u in range(cuts):
        share(u)
        for later in waiting[:2]:
            dispatch(later)
        del waiting[:2]
        multiply(u)
        reduce_step(u)
        done = u + 1
    for later in waiting:
        dispatch(later)


    for u in range(cuts, units, 2):
        pair = range(u, min(u + 2, units))
        for v in pair:
            share(v)
        for v in pair:
            multiply(v)
        for n in pair:
            if n < last:
                reduce_step(n)

    for n in range(last - 2 * cuts, last):
        right_finish(n, steps[n][2] == 0)
        left_finish(n, steps[n][2] == 0)

    for u in range(units):
        grad_copy(u).wait_send()
        sent = outgoing.at[u, pl.ds(0, n_chip - 1)]
        pltpu.make_async_copy(sent, sent, rows_send.at[u]).wait()
        share_copy(u).wait_send()
    for n in range(last):
        right_copy(n).wait_send()
        left_copy(n).wait_send()


def solution(mesh):
    sizes = (mesh.shape["pipe"], mesh.shape["dp"], mesh.shape["expert"] // 2)
    n_dp, n_chip = sizes[1:]

    def body(input_grad, gate_prob, expert_route, saved_hidden):
        tokens, width = input_grad.shape[1:]
        capacity, hidden_width = saved_hidden.shape[3:]
        rows = saved_hidden.shape[2] * capacity
        columns = 128
        units = width // columns
        half = columns // 2
        chain_steps = units - units // n_dp
        dma = pltpu.SemaphoreType.DMA
        in_place = pl.BlockSpec(memory_space=pltpu.MemorySpace.HBM)
        result = pl.pallas_call(
            functools.partial(kernel, sizes),
            out_shape=jax.ShapeDtypeStruct((1, width // n_dp, hidden_width), jnp.bfloat16),
            in_specs=[in_place] * 4,
            out_specs=pl.BlockSpec(memory_space=pltpu.VMEM),
            scratch_shapes=[
                pltpu.VMEM((units, tokens, columns), jnp.bfloat16),
                pltpu.VMEM((units, n_chip, capacity, columns), jnp.bfloat16),
                pltpu.VMEM((units, n_chip, 2, capacity, columns), jnp.bfloat16),
                pltpu.VMEM((units, columns, hidden_width), jnp.bfloat16),
                pltpu.VMEM((chain_steps, half, hidden_width), jnp.bfloat16),
                pltpu.VMEM((chain_steps, half, hidden_width), jnp.bfloat16),
                pltpu.VMEM((rows, hidden_width), jnp.bfloat16),
                pltpu.VMEM((1, tokens), jnp.float32),
                pltpu.VMEM((1, tokens), jnp.int32),
                pltpu.VMEM((n_chip * capacity, tokens), jnp.bfloat16),
                pltpu.VMEM((tokens, columns), jnp.float32),
                dma((3,)),
                *[dma((units,))] * 7,
                *[dma((chain_steps,))] * 4,
            ],
            compiler_params=pltpu.CompilerParams(
                collective_id=0, has_side_effects=True, vmem_limit_bytes=24 * 1024 * 1024
            ),
        )(
            *[
                pltpu.with_memory_space_constraint(value, pltpu.MemorySpace.HBM)
                for value in (
                    input_grad,
                    gate_prob,
                    expert_route.reshape(1, tokens),
                    saved_hidden.reshape(1, 1, rows, hidden_width),
                )
            ]
        )
        return result

    in_specs = (
        P("pipe", ("dp", "expert"), None),
        P("pipe", ("dp", "expert")),
        P("pipe", ("dp", "expert"), None),
        P("pipe", "dp", None, None, "expert"),
    )
    out_specs = P("pipe", "dp", "expert")
    return jax.shard_map(body, mesh=mesh, in_specs=in_specs, out_specs=out_specs, check_vma=False)
```

time: 94 us -> 91.5 us (0.973)
  Pallas kernels: 91.4 us -> 89.5 us
  local copies, waits for them, and re-layouts: 2.02 us -> 0.86 us
    pallas_call x1, Pallas kernels: 91.4 us -> 89.5 us  [body(): pl.pallas_call(functools.partial(kernel, sizes), out_shape=jax.ShapeDtype...]
    unnamed x1, local copies, waits for them, and re-layouts: 2.02 us -> 0.86 us
where the time goes in v2:
time: 91.5 us; the launch traced here: 90.4 us
  Pallas kernels  89.5 us (98%)
    pallas_call x1, Pallas kernels, body(): pl.pallas_call(functools.partial(kernel, sizes), out_shape=jax.ShapeDtype...  89.5 us

profile of v2, /device:TPU:1, one launch (start us, length us, event | category | flops | bytes accessed | tf_op | source)
XLA Modules:
  0.0 90.4 jit_solution(18205468529834674468)
XLA Ops:
  0.0 89.5 %shard_map.46 = bf16[1,256,1408]{2,1,0:T(8,128)(2,1)S(1)} custom-call(bf16[1,128,2048]{2,1,0:T(8,128)(2,1)} %grad_ref.1, f32[1,128]{1,0:T(1,128)} %prob_ref.1, s32[1,128]{1,0:T(1,128)} %bitcast.3, bf16[1,1,512,1408]{3,2,1,0:T(8,128)(2,1)} %bitcast.2), custom_call_target="tpu_custom_call" | custom-call | tf_op jit(solution)/shard_map/pallas_call | solution.py:296
  89.5 0.9 copy.6

commit v3 on v2

--- a/solution.py
+++ b/solution.py
@@ -29,6 +29,9 @@
     select,
     prob_column,
     local_sems,
+    wrap_sem,
+    ahead_sems,
+    behind_sems,
     grad_send,
     grad_recv,
     rows_send,
@@ -81,11 +84,28 @@
     route_copy.start()
 
     barrier = pltpu.get_barrier_semaphore()
-    partners = [right, left, sibling] + [peer(d) for d in range(1, n_chip)]
-
-    for partner in partners + [after]:
+    begins, ends = replica == 0, replica == n_dp - 1
+    partners = [after, left, sibling, peer(1), peer(n_chip - 1)]
+    for partner in partners:
         pl.semaphore_signal(barrier, inc=1, device_id=partner, device_id_type=MESH)
-    pl.semaphore_wait(barrier, len(partners) + 1)
+
+    @pl.when(jnp.logical_not(ends))
+    def _():
+        pl.semaphore_signal(barrier, inc=1, device_id=right, device_id_type=MESH)
+
+    pl.semaphore_wait(barrier, len(partners) + jnp.where(begins, 0, 1))
+
+    @pl.when(ends)
+    def _():
+        pl.semaphore_signal(wrap_sem, inc=1, device_id=right, device_id_type=MESH)
+
+    def tell(sems, distance, target):
+        pl.semaphore_signal(
+            sems.at[distance], inc=1, device_id=target, device_id_type=MESH
+        )
+
+    tell(ahead_sems, 2, peer(n_chip - 1))
+    tell(behind_sems, 2, peer(1))
 
     def grad_copy(u):
         distance, cut = order[u]
@@ -123,6 +143,15 @@
         jnp.sum(diagonal, axis=1, keepdims=True), prob_column.shape
     )
 
+    for distance in range(2, n_chip // 2 + 1):
+        pl.semaphore_wait(ahead_sems.at[distance], 1)
+        if distance < n_chip // 2:
+            tell(ahead_sems, distance + 1, peer(n_chip - 1))
+        if distance < n_chip // 2:
+            pl.semaphore_wait(behind_sems.at[distance], 1)
+            if distance + 1 < n_chip // 2:
+                tell(behind_sems, distance + 1, peer(1))
+
     def rows_copy(u, distance):
         return pltpu.make_async_remote_copy(
             src_ref=outgoing.at[u, on_chip(distance)],
@@ -183,6 +212,19 @@
                 )
     last = len(steps)
 
+    moved = cuts - 1
+
+    def moved_copy():
+        distance, cut, piece, _ = steps[moved]
+        return pltpu.make_async_remote_copy(
+            src_ref=part.at[order.index((distance, cut)), pl.ds(piece * half, half)],
+            dst_ref=from_right.at[last],
+            send_sem=left_send.at[last],
+            recv_sem=left_recv.at[last],
+            device_id=left,
+            device_id_type=MESH,
+        )
+
     def chain(side):
         to_right = side > 0
         send, recv = (right_send, right_recv) if to_right else (left_send, left_recv)
@@ -197,7 +239,7 @@
             return unit, row, source
 
         def copy(n):
-            unit, row, _ = place_of(n)
+            unit, row, _ = place_of(min(n, last - 1))
             return pltpu.make_async_remote_copy(
                 src_ref=part.at[unit, pl.ds(row, half)],
                 dst_ref=landing.at[n],
@@ -207,15 +249,30 @@
                 device_id_type=MESH,
             )
 
+        def add(unit, row, slot):
+            copy(slot).wait_recv()
+            part[unit, pl.ds(row, half)] = (
+                part[unit, pl.ds(row, half)].astype(jnp.float32)
+                + landing[slot].astype(jnp.float32)
+            ).astype(jnp.bfloat16)
+
         def advance(n):
             unit, row, source = place_of(n)
-            if source is not None:
-                copy(source).wait_recv()
-                part[unit, pl.ds(row, half)] = (
-                    part[unit, pl.ds(row, half)].astype(jnp.float32)
-                    + landing[source].astype(jnp.float32)
-                ).astype(jnp.bfloat16)
-            copy(n).start()
+            if to_right and source == moved:
+                pl.when(jnp.logical_not(begins))(lambda: add(unit, row, source))
+            elif source is not None:
+                add(unit, row, source)
+            elif not to_right and (steps[n][0], steps[n][1], 1 - steps[n][2]) == (
+                far - 1,
+                steps[moved][1],
+                steps[moved][2],
+            ):
+                pl.when(replica == n_dp - 2)(lambda: add(unit, row, last))
+            if to_right and n == moved:
+                pl.when(jnp.logical_not(ends))(lambda: copy(n).start())
+                pl.when(ends)(lambda: moved_copy().start())
+            else:
+                copy(n).start()
 
         def finish(n, to_out):
             unit, row, _ = place_of(n, closer=1)
@@ -235,6 +292,8 @@
 
     def reduce_step(n):
         right_advance(n)
+        if n == 0:
+            pl.when(begins)(lambda: pl.semaphore_wait(wrap_sem, 1))
         left_advance(n)
 
     for u in range(units // 2):
@@ -275,7 +334,11 @@
         pltpu.make_async_copy(sent, sent, rows_send.at[u]).wait()
         share_copy(u).wait_send()
     for n in range(last):
-        right_copy(n).wait_send()
+        if n == moved:
+            pl.when(jnp.logical_not(ends))(lambda: right_copy(moved).wait_send())
+            pl.when(ends)(lambda: moved_copy().wait_send())
+        else:
+            right_copy(n).wait_send()
         left_copy(n).wait_send()
 
 
@@ -304,15 +367,18 @@
                 pltpu.VMEM((units, n_chip, 2, capacity, columns), jnp.bfloat16),
                 pltpu.VMEM((units, columns, hidden_width), jnp.bfloat16),
                 pltpu.VMEM((chain_steps, half, hidden_width), jnp.bfloat16),
-                pltpu.VMEM((chain_steps, half, hidden_width), jnp.bfloat16),
+                pltpu.VMEM((chain_steps + 1, half, hidden_width), jnp.bfloat16),
                 pltpu.VMEM((rows, hidden_width), jnp.bfloat16),
                 pltpu.VMEM((1, tokens), jnp.float32),
                 pltpu.VMEM((1, tokens), jnp.int32),
                 pltpu.VMEM((n_chip * capacity, tokens), jnp.bfloat16),
                 pltpu.VMEM((tokens, columns), jnp.float32),
                 dma((3,)),
+                pltpu.SemaphoreType.REGULAR,
+                pltpu.SemaphoreType.REGULAR((n_chip // 2 + 1,)),
+                pltpu.SemaphoreType.REGULAR((n_chip // 2 + 1,)),
                 *[dma((units,))] * 7,
-                *[dma((chain_steps,))] * 4,
+                *[dma((chain_steps + 1,))] * 4,
             ],
             compiler_params=pltpu.CompilerParams(
                 collective_id=0, has_side_effects=True, vmem_limit_bytes=24 * 1024 * 1024

time: 91.5 us -> 88 us (0.962)
  Pallas kernels: 89.5 us -> 86.9 us
    pallas_call x1, Pallas kernels: 89.5 us -> 86.9 us  [body(): pl.pallas_call(functools.partial(kernel, sizes), out_shape=jax.ShapeDtype...]
where the time goes in v3:
time: 88 us; the launch traced here: 87.8 us
  Pallas kernels  86.9 us (99%)
    pallas_call x1, Pallas kernels, body(): pl.pallas_call(functools.partial(kernel, sizes), out_shape=jax.ShapeDtype...  86.9 us

profile of v3, /device:TPU:1, one launch (start us, length us, event | category | flops | bytes accessed | tf_op | source)
XLA Modules:
  0.0 87.8 jit_solution(15207117052651788003)
XLA Ops:
  0.0 86.9 %shard_map.46 = bf16[1,256,1408]{2,1,0:T(8,128)(2,1)S(1)} custom-call(bf16[1,128,2048]{2,1,0:T(8,128)(2,1)} %grad_ref.1, f32[1,128]{1,0:T(1,128)} %prob_ref.1, s32[1,128]{1,0:T(1,128)} %bitcast.3, bf16[1,1,512,1408]{3,2,1,0:T(8,128)(2,1)} %bitcast.2), custom_call_target="tpu_custom_call" | custom-call | tf_op jit(solution)/shard_map/pallas_call | solution.py:359
  86.9 0.9 copy.6

commit v4 on v3

--- a/solution.py
+++ b/solution.py
@@ -71,8 +71,10 @@
     def peer(distance):
         return {"expert": on_chip(distance) * 2 + core}
 
-    order = [(far, cut) for cut in range(cuts)]
-    for distance in range(far - 1, 0, -1):
+    order = []
+    for cut in range(cuts):
+        order += [(far, cut), (far - 1, cut), (1 - far, cut)]
+    for distance in range(far - 2, 0, -1):
         order += [(side * distance, cut) for cut in range(cuts) for side in (1, -1)]
     order += [(0, cut) for cut in range(cuts)]
 
@@ -201,26 +203,29 @@
             rows, hidden[...], (((0,), (0,)), ((), ())), preferred_element_type=jnp.float32
         ).astype(jnp.bfloat16)
 
-    steps = [(far, cut, 0, None) for cut in range(cuts)]
-    for distance in range(far - 1, 0, -1):
-        for cut in range(cuts):
-            for piece in (1, 0):
-                source = (distance + 1, cut, piece)
-                known = [step[:3] for step in steps]
-                steps.append(
-                    (distance, cut, piece, known.index(source) if source in known else None)
-                )
+    plan = [(far, 0, 0), (far - 1, 0, 1)]
+    for cut in range(1, cuts):
+        plan += [(far, cut, 0), (far - 1, cut - 1, 0), (far - 1, cut, 1)]
+    plan.append((far - 1, cuts - 1, 0))
+    for distance in range(far - 2, 0, -1):
+        plan += [(distance, cut, piece) for cut in range(cuts) for piece in (1, 0)]
+    steps = []
+    for distance, cut, piece in plan:
+        source = (distance + 1, cut, piece)
+        steps.append(
+            (distance, cut, piece, plan.index(source) if source in plan else None)
+        )
     last = len(steps)
 
-    moved = cuts - 1
-
-    def moved_copy():
-        distance, cut, piece, _ = steps[moved]
+    moved_rows = [half * 3 // 4] + [half] * (cuts - 1)
+
+    def moved_copy(cut):
+        rows = pl.ds(0, moved_rows[cut])
         return pltpu.make_async_remote_copy(
-            src_ref=part.at[order.index((distance, cut)), pl.ds(piece * half, half)],
-            dst_ref=from_right.at[last],
-            send_sem=left_send.at[last],
-            recv_sem=left_recv.at[last],
+            src_ref=part.at[order.index((far, cut)), rows],
+            dst_ref=from_right.at[last + cut, rows],
+            send_sem=left_send.at[last + cut],
+            recv_sem=left_recv.at[last + cut],
             device_id=left,
             device_id_type=MESH,
         )
@@ -238,39 +243,45 @@
             row = (piece if to_right else 1 - piece) * half
             return unit, row, source
 
-        def copy(n):
+        def copy(n, offset=0, rows=half):
             unit, row, _ = place_of(min(n, last - 1))
             return pltpu.make_async_remote_copy(
-                src_ref=part.at[unit, pl.ds(row, half)],
-                dst_ref=landing.at[n],
+                src_ref=part.at[unit, pl.ds(row + offset, rows)],
+                dst_ref=landing.at[n, pl.ds(offset, rows)],
                 send_sem=send.at[n],
                 recv_sem=recv.at[n],
                 device_id=target,
                 device_id_type=MESH,
             )
 
-        def add(unit, row, slot):
-            copy(slot).wait_recv()
-            part[unit, pl.ds(row, half)] = (
-                part[unit, pl.ds(row, half)].astype(jnp.float32)
-                + landing[slot].astype(jnp.float32)
+        def add(unit, row, slot, offset=0, rows=half):
+            copy(slot, offset, rows).wait_recv()
+            span = pl.ds(row + offset, rows)
+            part[unit, span] = (
+                part[unit, span].astype(jnp.float32)
+                + landing[slot, pl.ds(offset, rows)].astype(jnp.float32)
             ).astype(jnp.bfloat16)
 
         def advance(n):
             unit, row, source = place_of(n)
-            if to_right and source == moved:
+            distance, cut, piece, _ = steps[n]
+            if to_right and source is not None and distance == far - 1:
+                kept = half - moved_rows[cut]
                 pl.when(jnp.logical_not(begins))(lambda: add(unit, row, source))
+                if kept:
+                    pl.when(begins)(lambda: add(unit, row, source, half - kept, kept))
             elif source is not None:
                 add(unit, row, source)
-            elif not to_right and (steps[n][0], steps[n][1], 1 - steps[n][2]) == (
-                far - 1,
-                steps[moved][1],
-                steps[moved][2],
-            ):
-                pl.when(replica == n_dp - 2)(lambda: add(unit, row, last))
-            if to_right and n == moved:
+            elif not to_right and distance == far - 1:
+                pl.when(replica == n_dp - 2)(
+                    lambda: add(unit, row, last + cut, 0, moved_rows[cut])
+                )
+            if to_right and distance == far:
+                kept = half - moved_rows[cut]
                 pl.when(jnp.logical_not(ends))(lambda: copy(n).start())
-                pl.when(ends)(lambda: moved_copy().start())
+                if kept:
+                    pl.when(ends)(lambda: copy(n, half - kept, kept).start())
+                pl.when(ends)(lambda: moved_copy(cut).start())
             else:
                 copy(n).start()
 
@@ -290,39 +301,41 @@
     right_copy, right_advance, right_finish = chain(1)
     left_copy, left_advance, left_finish = chain(-1)
 
-    def reduce_step(n):
-        right_advance(n)
-        if n == 0:
-            pl.when(begins)(lambda: pl.semaphore_wait(wrap_sem, 1))
-        left_advance(n)
-
-    for u in range(units // 2):
-        dispatch(u)
-        if u == 0:
-            hidden_copy.wait()
-    waiting = list(range(units // 2, units))
-    done = 0
-    for u in range(cuts):
+    ahead = list(range(units))
+    to_send = {1: list(range(last)), -1: list(range(last))}
+
+    def dispatch_next(count):
+        for u in ahead[:count]:
+            dispatch(u)
+        del ahead[:count]
+
+    def send_made(u):
+        for n in range(u + 1):
+            for side, advance in ((1, right_advance), (-1, left_advance)):
+                distance = steps[n][0] if n < last else 0
+                unit = (distance if distance == far else side * distance, steps[n % last][1])
+                if n in to_send[side] and order.index(unit) <= u:
+                    if n == 0 and side < 0:
+                        pl.when(begins)(lambda: pl.semaphore_wait(wrap_sem, 1))
+                    advance(n)
+                    to_send[side].remove(n)
+
+    dispatch_next(1)
+    hidden_copy.wait()
+    dispatch_next(3)
+    for u in range(4):
         share(u)
-        for later in waiting[:2]:
-            dispatch(later)
-        del waiting[:2]
+        dispatch_next(2 if u < 2 else 1)
         multiply(u)
-        reduce_step(u)
-        done = u + 1
-    for later in waiting:
-        dispatch(later)
-
-
-    for u in range(cuts, units, 2):
-        pair = range(u, min(u + 2, units))
-        for v in pair:
-            share(v)
-        for v in pair:
-            multiply(v)
-        for n in pair:
-            if n < last:
-                reduce_step(n)
+        send_made(u)
+    for u in range(4, units, 2):
+        share(u)
+        share(u + 1)
+        dispatch_next(2)
+        multiply(u)
+        send_made(u)
+        multiply(u + 1)
+        send_made(u + 1)
 
     for n in range(last - 2 * cuts, last):
         right_finish(n, steps[n][2] == 0)
@@ -334,9 +347,13 @@
         pltpu.make_async_copy(sent, sent, rows_send.at[u]).wait()
         share_copy(u).wait_send()
     for n in range(last):
-        if n == moved:
-            pl.when(jnp.logical_not(ends))(lambda: right_copy(moved).wait_send())
-            pl.when(ends)(lambda: moved_copy().wait_send())
+        distance, cut = steps[n][:2]
+        if distance == far:
+            kept = half - moved_rows[cut]
+            pl.when(jnp.logical_not(ends))(lambda: right_copy(n).wait_send())
+            if kept:
+                pl.when(ends)(lambda: right_copy(n, half - kept, kept).wait_send())
+            pl.when(ends)(lambda: moved_copy(cut).wait_send())
         else:
             right_copy(n).wait_send()
         left_copy(n).wait_send()
@@ -367,7 +384,7 @@
                 pltpu.VMEM((units, n_chip, 2, capacity, columns), jnp.bfloat16),
                 pltpu.VMEM((units, columns, hidden_width), jnp.bfloat16),
                 pltpu.VMEM((chain_steps, half, hidden_width), jnp.bfloat16),
-                pltpu.VMEM((chain_steps + 1, half, hidden_width), jnp.bfloat16),
+                pltpu.VMEM((chain_steps + units // n_dp, half, hidden_width), jnp.bfloat16),
                 pltpu.VMEM((rows, hidden_width), jnp.bfloat16),
                 pltpu.VMEM((1, tokens), jnp.float32),
                 pltpu.VMEM((1, tokens), jnp.int32),
@@ -378,7 +395,7 @@
                 pltpu.SemaphoreType.REGULAR((n_chip // 2 + 1,)),
                 pltpu.SemaphoreType.REGULAR((n_chip // 2 + 1,)),
                 *[dma((units,))] * 7,
-                *[dma((chain_steps + 1,))] * 4,
+                *[dma((chain_steps + units // n_dp,))] * 4,
             ],
             compiler_params=pltpu.CompilerParams(
                 collective_id=0, has_side_effects=True, vmem_limit_bytes=24 * 1024 * 1024

time: 88 us -> 85 us (0.966)
  Pallas kernels: 86.9 us -> 84 us
    pallas_call x1, Pallas kernels: 86.9 us -> 84 us  [body(): pl.pallas_call(functools.partial(kernel, sizes), out_shape=jax.ShapeDtype...]
where the time goes in v4:
time: 85 us; the launch traced here: 84.9 us
  Pallas kernels  84 us (99%)
  local copies, waits for them, and re-layouts  0.86 us (1%)
    pallas_call x1, Pallas kernels, body(): pl.pallas_call(functools.partial(kernel, sizes), out_shape=jax.ShapeDtype...  84 us

profile of v4, /device:TPU:1, one launch (start us, length us, event | category | flops | bytes accessed | tf_op | source)
XLA Modules:
  0.0 84.9 jit_solution(9138119083160051696)
XLA Ops:
  0.0 84.0 %shard_map.46 = bf16[1,256,1408]{2,1,0:T(8,128)(2,1)S(1)} custom-call(bf16[1,128,2048]{2,1,0:T(8,128)(2,1)} %grad_ref.1, f32[1,128]{1,0:T(1,128)} %prob_ref.1, s32[1,128]{1,0:T(1,128)} %bitcast.3, bf16[1,1,512,1408]{3,2,1,0:T(8,128)(2,1)} %bitcast.2), custom_call_target="tpu_custom_call" | custom-call | tf_op jit(solution)/shard_map/pallas_call | solution.py:376
  84.0 0.9 %copy.6 = bf16[1,256,1408]{2,1,0:T(8,128)(2,1)} copy(bf16[1,256,1408]{2,1,0:T(8,128)(2,1)S(1)} %shard_map.46) | data formatting | bytes 1441792

commit v5 on v4

--- a/solution.py
+++ b/solution.py
@@ -323,13 +323,16 @@
     dispatch_next(1)
     hidden_copy.wait()
     dispatch_next(3)
+    share(0)
+    dispatch_next(1)
     for u in range(4):
-        share(u)
-        dispatch_next(2 if u < 2 else 1)
+        share(u + 1)
         multiply(u)
         send_made(u)
+        dispatch_next(2 if u < 1 else 1)
     for u in range(4, units, 2):
-        share(u)
+        if u > 4:
+            share(u)
         share(u + 1)
         dispatch_next(2)
         multiply(u)

time: 85 us -> 84.8 us (level)
  no operation moved by 1% of the time
where the time goes in v5:
time: 84.8 us; the launch traced here: 84.7 us
  Pallas kernels  83.8 us (99%)
  local copies, waits for them, and re-layouts  0.86 us (1%)
    pallas_call x1, Pallas kernels, body(): pl.pallas_call(functools.partial(kernel, sizes), out_shape=jax.ShapeDtype...  83.8 us

profile of v5, /device:TPU:1, one launch (start us, length us, event | category | flops | bytes accessed | tf_op | source)
XLA Modules:
  0.0 84.7 jit_solution(15863406876485219207)
XLA Ops:
  0.0 83.8 %shard_map.46 = bf16[1,256,1408]{2,1,0:T(8,128)(2,1)S(1)} custom-call(bf16[1,128,2048]{2,1,0:T(8,128)(2,1)} %grad_ref.1, f32[1,128]{1,0:T(1,128)} %prob_ref.1, s32[1,128]{1,0:T(1,128)} %bitcast.3, bf16[1,1,512,1408]{3,2,1,0:T(8,128)(2,1)} %bitcast.2), custom_call_target="tpu_custom_call" | custom-call | tf_op jit(solution)/shard_map/pallas_call | solution.py:379
  83.8 0.9 %copy.6 = bf16[1,256,1408]{2,1,0:T(8,128)(2,1)} copy(bf16[1,256,1408]{2,1,0:T(8,128)(2,1)S(1)} %shard_map.46) | data formatting | bytes 1441792
